TPU v7x, 32 devices: a whole 2x2x4 slice. The times are simulated.
32 devices in a mesh: win: 2 (over x), wide: 8 (over z, y), narrow: 2 (over core).
Axes of the slice: x: 2, y: 2, z: 4, core: 2. Of those that a mesh axis runs over, the one named last changes fastest.
Arguments:
- window_data: float32 [384, 128, 256], P(('win', 'wide'), 'narrow'), parts along dimension 0, may hold values from -6 to 6
- factor_one: float32 [256, 48], P(('win', 'narrow')), parts along dimension 0, may hold values from -0.5 to 0.5
- factor_two: float32 [512, 48], P('win'), parts along dimension 0, may hold values from -0.375 to 0.375
- factor_three: float32 [384, 48], P(('win', 'wide')), parts along dimension 0, may hold values from -0.4375 to 0.4375
Outputs:
- basis_one: float32 [256, 48], P(('win', 'narrow')), parts along dimension 0
- basis_two: float32 [512, 48], P('win'), parts along dimension 0
- basis_three: float32 [384, 48], P(('win', 'wide')), parts along dimension 0
- core_unfolded: float32 [48, 4608], P(None, ('win', 'wide', 'narrow')), parts along dimension 1
There are 2 independent parts, one for each index of `win`. A program takes and returns all parts, laid end to end along the dimension named above; each array names one. Nothing has to cross between parts.
All inputs are finite; a program needn't handle non-finite values.
Results may differ from a plain program's by a relative error of at most 0.0003.
Values sent between devices are 32-bit elements; how exact they have to be, the bound alone decides.
No kernel may reach another device: no remote copies, remote signals or barrier semaphores. Data moves between devices by JAX's collectives and lax.ppermute only.
A program may use at most 64 MiB of HBM per device.

v0:
```python
import jax
import jax.numpy as jnp
from jax import lax
from jax.sharding import PartitionSpec as P

highest = lax.Precision.HIGHEST


def contract(form, left, right):
    return jnp.einsum(form, left, right, precision=highest)


def orthonormal(basis, gram):
    lower = jnp.linalg.cholesky(gram)
    return lax.linalg.triangular_solve(lower, basis, left_side=False, lower=True, transpose_a=True)


def full_core(partial_value):
    flat = partial_value.reshape(
        partial_value.shape[0], partial_value.shape[1] * partial_value.shape[2]
    )
    shares = lax.psum_scatter(flat, ("wide", "narrow"), scatter_dimension=1, tiled=True)
    whole = lax.all_gather(shares, ("wide", "narrow"), axis=1, tiled=True)
    return whole.reshape(partial_value.shape)


def on_device(window_data, factor_one, factor_two, factor_three):
    rank = factor_one.shape[1]
    along_two = contract("kij,jb->kib", window_data, factor_two)
    unfold_part = contract("kib,kc->ibc", along_two, factor_three).reshape(
        along_two.shape[1], rank * rank
    )
    unfold_rows = lax.psum_scatter(unfold_part, "wide", scatter_dimension=1, tiled=True)
    weights_one = lax.psum(jnp.dot(unfold_rows.T, factor_one, precision=highest), "narrow")
    product_one = lax.psum(jnp.dot(unfold_rows, weights_one, precision=highest), "wide")
    gram_one = lax.psum(jnp.dot(product_one.T, product_one, precision=highest), "narrow")
    basis_one = orthonormal(product_one, gram_one)
    along_one = contract("kij,ia->kaj", window_data, basis_one)
    core_two = full_core(
        contract("kab,kc->abc", contract("kaj,jb->kab", along_one, factor_two), factor_three)
    )
    spread_two = contract("abc,kc->kab", core_two, factor_three)
    product_two = lax.psum(contract("kaj,kab->jb", along_one, spread_two), ("wide", "narrow"))
    basis_two = orthonormal(product_two, jnp.dot(product_two.T, product_two, precision=highest))
    along_new = contract("kij,jb->kib", window_data, basis_two)
    unfold_three = contract("kib,ia->kab", along_new, basis_one)
    core_three = full_core(contract("kab,kc->abc", unfold_three, factor_three))
    product_three = lax.psum(contract("kab,abc->kc", unfold_three, core_three), "narrow")
    gram_three = lax.psum(jnp.dot(product_three.T, product_three, precision=highest), "wide")
    basis_three = orthonormal(product_three, gram_three)
    core_part = contract("kab,kc->abc", unfold_three, basis_three).reshape(rank, rank * rank)
    core_shares = lax.psum_scatter(core_part, ("wide", "narrow"), scatter_dimension=1, tiled=True)
    return (basis_one, basis_two, basis_three, core_shares)


def solution(mesh):
    return jax.shard_map(
        on_device,
        mesh=mesh,
        in_specs=(
            P(("win", "wide"), "narrow", None),
            P(("win", "narrow"), None),
            P("win", None),
            P(("win", "wide"), None),
        ),
        out_specs=(
            P(("win", "narrow"), None),
            P("win", None),
            P(("win", "wide"), None),
            P(None, ("win", "wide", "narrow")),
        ),
        check_vma=False,
    )
```

profile of v0, /device:TPU:0, one launch (start us, length us, event | category | flops | bytes accessed | tf_op | source)
XLA Modules:
  0.0 505.6 jit_solution(5925950153966513324)
XLA Ops:
  8.6 3.1 fusion.12
  11.7 2.2 fusion.3
  13.9 67.9 %reduce-scatter.11.cloned.1.call-done = f32[64,288]{0,1:T(8,128)} async-done(((f32[64,2304]{0,1:T(8,128)}), f32[64,288]{0,1:T(8,128)}) %reduce-scatter.11.cloned.1.call-update) | async-done | bytes 73744 | tf_op jit(solution)/shard_map/reduce_scatter | solution.py:33
  83.1 3.5 psum.42
  87.7 34.9 %psum.43 = f32[64,48]{0,1:T(8,128)S(1)} all-reduce(f32[64,48]{0,1:T(8,128)S(1)} %fusion.35), channel_id=1, replica_groups=mesh['win'=2,'wide'=8,'narrow'=2] {'wide'}, use_global_device_ids=true, to_apply=%region_2.0 | all-reduce | flops 3072 | bytes 24576 | tf_op jit(solution)/shard_map/psum | solution.py:35
  122.8 3.4 psum.44
  126.3 4.4 cholesky.59
  132.0 3.7 custom-call.11
  137.1 1.6 fusion
  138.7 3.1 fusion.31
  141.8 2.7 copy.45
  144.6 55.5 %reduce-scatter.13.cloned.1.call-done = f32[144,48]{1,0:T(8,128)} async-done(((f32[2304,48]{1,0:T(8,128)}), f32[144,48]{1,0:T(8,128)}) %reduce-scatter.13.cloned.1.call-update) | async-done | bytes 27664
  201.0 21.8 %all-gather = f32[16,144,48]{1,2,0:T(8,128)S(1)} all-gather(f32[1,144,48]{1,2,0:T(8,128)S(1)} %bitcast.116), channel_id=1, replica_groups=mesh['win'=2,'wide'=8,'narrow'=2] {'wide','narrow'}, dimensions={0}, use_global_device_ids=true | all-gather | bytes 470016 | tf_op jit(solution)/shard_map/all_gather | solution.py:23
  224.4 2.7 reshape.42
  227.2 4.7 convolution_bitcast_fusion.3
  233.1 57.9 %psum.45 = f32[256,48]{0,1:T(8,128)S(1)} all-reduce(f32[256,48]{0,1:T(8,128)S(1)} %convolution_bitcast_fusion.4), channel_id=1, replica_groups=mesh['win'=2,'wide'=8,'narrow'=2] {'wide','narrow'}, use_global_device_ids=true, to_apply=%region_7.0 | all-reduce | flops 12288 | bytes 98304 | tf_op jit(solution)/shard_map/psum | solution.py:43
  291.3 4.4 cholesky.70
  297.0 3.7 custom-call.12
  301.0 2.3 convolution_bitcast_fusion.2
  303.3 2.1 convolution_bitcast_fusion.1
  305.5 2.0 fusion.7
  307.5 1.5 copy.46
  309.1 55.5 %reduce-scatter.15.cloned.1.call-done = f32[144,48]{1,0:T(8,128)} async-done(((f32[2304,48]{1,0:T(8,128)}), f32[144,48]{1,0:T(8,128)}) %reduce-scatter.15.cloned.1.call-update) | async-done | bytes 27664
  365.5 21.8 %all-gather.1 = f32[16,144,48]{1,2,0:T(8,128)S(1)} all-gather(f32[1,144,48]{1,2,0:T(8,128)S(1)} %bitcast.117), channel_id=1, replica_groups=mesh['win'=2,'wide'=8,'narrow'=2] {'wide','narrow'}, dimensions={0}, use_global_device_ids=true | all-gather | bytes 470016 | tf_op jit(solution)/shard_map/all_gather | solution.py:23
  388.9 1.7 reshape.44
  391.9 3.5 psum.46
  395.6 33.0 %psum.47 = f32[48,48]{0,1:T(8,128)S(1)} all-reduce(f32[48,48]{0,1:T(8,128)S(1)} %fusion.38), channel_id=1, replica_groups=mesh['win'=2,'wide'=8,'narrow'=2] {'wide'}, use_global_device_ids=true, to_apply=%region_10.12 | all-reduce | flops 2304 | bytes 18432 | tf_op jit(solution)/shard_map/psum | solution.py:49
  428.7 4.4 cholesky.81
  434.4 3.7 custom-call.13
  438.3 2.0 fusion.5
  441.9 55.6 %reduce-scatter.17.cloned.1.call-done = f32[144,48]{1,0:T(8,128)} async-done(((f32[2304,48]{1,0:T(8,128)}), f32[144,48]{1,0:T(8,128)}) %reduce-scatter.17.cloned.1.call-update) | async-done | bytes 27664
  497.5 1.6 copy.44
  (57 shorter events, 19.5 us)
Async XLA Ops:
  7.2 1.4 copy-start
  7.2 4.5 copy-start.3
  7.2 74.7 %reduce-scatter.11.cloned.1.call-start = ((), (), s32[]{:S(2)}) async-start(), calls=%async_computation.4 | async-start | bytes 1327104 | tf_op jit(solution)/shard_map/reduce_scatter | solution.py:33
  11.7 70.2 %copy-start.7 = (f32[64,48]{0,1:T(8,128)S(1)}, f32[64,48]{0,1:T(8,128)}, u32[]{:S(2)}) copy-start(f32[64,48]{0,1:T(8,128)} %param.6) | copy-start | bytes 36868
  13.9 186.2 %reduce-scatter.13.cloned.1.call-start = ((), (), s32[]{:S(2)}) async-start(), calls=%async_computation.5 | async-start | bytes 1253376
  135.9 1.1 copy-start.1
  136.0 1.1 copy-start.5
  144.5 220.0 %reduce-scatter.15.cloned.1.call-start = ((), (), s32[]{:S(2)}) async-start(), calls=%async_computation.6 | async-start | bytes 1253376
  297.0 6.3 %copy-start.2 = (f32[64,48]{0,1:T(8,128)S(1)}, f32[64,48]{0,1:T(8,128)}, u32[]{:S(2)}) copy-start(f32[64,48]{0,1:T(8,128)} %copy-done.1) | copy-start | bytes 36868
  301.0 4.5 copy-start.4
  309.0 188.4 %reduce-scatter.17.cloned.1.call-start = ((), (), s32[]{:S(2)}) async-start(), calls=%async_computation.7 | async-start | bytes 1253376
  438.3 3.6 copy-start.6
Sparse Core Ops, SparseCore 0:
  14.0 67.8 reduce-scatter.10
  144.7 55.3 reduce-scatter.12
  309.1 55.3 reduce-scatter.14
  442.0 55.4 reduce-scatter.16
where the time goes:
time: 506 us
  waiting for transfers between devices  235 us (46%)
  blocking collectives  180 us (36%)
  matrix products  30.3 us (6%)
  other arithmetic  28.2 us (6%)
  local copies, waits for them, and re-layouts  18.5 us (4%)
  between operations  14.1 us (3%)
    unnamed x7, waiting for transfers between devices  167 us
    reduce_scatter x1, waiting for transfers between devices, on_device(): lax.psum_scatter(unfold_part, 'wide', scatter_dimension=1, tiled=True)  67.9 us
    psum x1, blocking collectives, on_device(): lax.psum(contract('kaj,kab->jb', along_one, spread_two), ('wide', 'narrow'))  57.9 us
    all_gather x2, blocking collectives, full_core(): whole = lax.all_gather(shares, ('wide', 'narrow'), axis=1, tiled=True)  43.6 us
    psum x1, blocking collectives, on_device(): lax.psum(jnp.dot(unfold_rows, weights_one, precision=highest), 'wide')  34.9 us
    psum x1, blocking collectives, on_device(): lax.psum(jnp.dot(product_three.T, product_three, precision=highest), 'wide')  33 us
    dot_general x12, matrix products, contract(): return jnp.einsum(form, left, right, precision=highest)  26.7 us
    another operation x9, other arithmetic, orthonormal(): lower = jnp.linalg.cholesky(gram)  15.2 us
  transfers between devices with their start and end apart: 4, of which 4 were waited for; matrix products, arithmetic and copies ran while one was open for 0% of the time, Pallas kernels for 0%

commit v1 on v0

--- a/solution.py
+++ b/solution.py
@@ -40,7 +40,9 @@
         contract("kab,kc->abc", contract("kaj,jb->kab", along_one, factor_two), factor_three)
     )
     spread_two = contract("abc,kc->kab", core_two, factor_three)
-    product_two = lax.psum(contract("kaj,kab->jb", along_one, spread_two), ("wide", "narrow"))
+    product_two = lax.psum(
+        lax.psum(contract("kaj,kab->jb", along_one, spread_two), "narrow"), "wide"
+    )
     basis_two = orthonormal(product_two, jnp.dot(product_two.T, product_two, precision=highest))
     along_new = contract("kij,jb->kib", window_data, basis_two)
     unfold_three = contract("kib,ia->kab", along_new, basis_one)

time: 506 us -> 487 us (0.962)
  blocking collectives: 180 us -> 159 us
    psum x1 -> x2, blocking collectives: 57.9 us -> 37.1 us  [the longest x1 33.4 us: on_device(): lax.psum(lax.psum(contract('kaj,kab->jb', along_one, spread_two), 'narrow...]
where the time goes in v1:
time: 487 us; the launch traced here: 486 us
  waiting for transfers between devices  236 us (48%)
  blocking collectives  159 us (33%)
  matrix products  30.3 us (6%)
  other arithmetic  28.2 us (6%)
  local copies, waits for them, and re-layouts  18.5 us (4%)
  between operations  14.1 us (3%)
    unnamed x7, waiting for transfers between devices  168 us
    reduce_scatter x1, waiting for transfers between devices, on_device(): lax.psum_scatter(unfold_part, 'wide', scatter_dimension=1, tiled=True)  67.9 us
    all_gather x2, blocking collectives, full_core(): whole = lax.all_gather(shares, ('wide', 'narrow'), axis=1, tiled=True)  43.4 us
    psum x1, blocking collectives, on_device(): lax.psum(jnp.dot(unfold_rows, weights_one, precision=highest), 'wide')  34.9 us
    psum x1, blocking collectives, on_device(): lax.psum(lax.psum(contract('kaj,kab->jb', along_one, spread_two), 'narrow...  33.4 us
    psum x1, blocking collectives, on_device(): lax.psum(jnp.dot(product_three.T, product_three, precision=highest), 'wide')  33 us
    dot_general x12, matrix products, contract(): return jnp.einsum(form, left, right, precision=highest)  26.7 us
    another operation x9, other arithmetic, orthonormal(): lower = jnp.linalg.cholesky(gram)  15.2 us
  transfers between devices with their start and end apart: 4, of which 4 were waited for; matrix products, arithmetic and copies ran while one was open for 0% of the time, Pallas kernels for 0%

profile of v1, /device:TPU:0, one launch (start us, length us, event | category | flops | bytes accessed | tf_op | source)
XLA Modules:
  0.0 486.0 jit_solution(8876660229233919853)
XLA Ops:
  8.6 3.1 fusion.12
  11.7 2.2 fusion.3
  13.9 67.9 %reduce-scatter.11.cloned.1.call-done = f32[64,288]{0,1:T(8,128)} async-done(((f32[64,2304]{0,1:T(8,128)}), f32[64,288]{0,1:T(8,128)}) %reduce-scatter.11.cloned.1.call-update) | async-done | bytes 73744 | tf_op jit(solution)/shard_map/reduce_scatter | solution.py:33
  83.1 3.5 psum.49
  87.7 34.9 %psum.50 = f32[64,48]{0,1:T(8,128)S(1)} all-reduce(f32[64,48]{0,1:T(8,128)S(1)} %fusion.35), channel_id=1, replica_groups=mesh['win'=2,'wide'=8,'narrow'=2] {'wide'}, use_global_device_ids=true, to_apply=%region_2.0 | all-reduce | flops 3072 | bytes 24576 | tf_op jit(solution)/shard_map/psum | solution.py:35
  122.8 3.4 psum.51
  126.3 4.4 cholesky.59
  132.0 3.7 custom-call.11
  137.1 1.6 fusion
  138.7 3.1 fusion.31
  141.8 2.7 copy.45
  144.6 55.5 %reduce-scatter.13.cloned.1.call-done = f32[144,48]{1,0:T(8,128)} async-done(((f32[2304,48]{1,0:T(8,128)}), f32[144,48]{1,0:T(8,128)}) %reduce-scatter.13.cloned.1.call-update) | async-done | bytes 27664
  201.0 21.8 %all-gather = f32[16,144,48]{1,2,0:T(8,128)S(1)} all-gather(f32[1,144,48]{1,2,0:T(8,128)S(1)} %bitcast.116), channel_id=1, replica_groups=mesh['win'=2,'wide'=8,'narrow'=2] {'wide','narrow'}, dimensions={0}, use_global_device_ids=true | all-gather | bytes 470016 | tf_op jit(solution)/shard_map/all_gather | solution.py:23
  224.4 2.7 reshape.42
  227.2 4.7 convolution_bitcast_fusion.3
  233.1 3.7 psum.52
  236.8 33.4 %psum.53 = f32[256,48]{0,1:T(8,128)S(1)} all-reduce(f32[256,48]{0,1:T(8,128)S(1)} %psum.52), channel_id=1, replica_groups=mesh['win'=2,'wide'=8,'narrow'=2] {'wide'}, use_global_device_ids=true, to_apply=%region_8.0 | all-reduce | flops 12288 | bytes 98304 | tf_op jit(solution)/shard_map/psum | solution.py:43
  270.5 4.4 cholesky.70
  276.2 3.7 custom-call.12
  280.2 2.3 convolution_bitcast_fusion.2
  282.5 2.1 convolution_bitcast_fusion.1
  284.7 2.0 fusion.7
  288.5 56.7 %reduce-scatter.15.cloned.1.call-done = f32[144,48]{1,0:T(8,128)} async-done(((f32[2304,48]{1,0:T(8,128)}), f32[144,48]{1,0:T(8,128)}) %reduce-scatter.15.cloned.1.call-update) | async-done | bytes 27664
  346.1 21.6 %all-gather.1 = f32[16,144,48]{1,2,0:T(8,128)S(1)} all-gather(f32[1,144,48]{1,2,0:T(8,128)S(1)} %bitcast.117), channel_id=1, replica_groups=mesh['win'=2,'wide'=8,'narrow'=2] {'wide','narrow'}, dimensions={0}, use_global_device_ids=true | all-gather | bytes 470016 | tf_op jit(solution)/shard_map/all_gather | solution.py:23
  369.3 1.7 reshape.44
  372.3 3.5 psum.54
  376.0 33.0 %psum.55 = f32[48,48]{0,1:T(8,128)S(1)} all-reduce(f32[48,48]{0,1:T(8,128)S(1)} %fusion.38), channel_id=1, replica_groups=mesh['win'=2,'wide'=8,'narrow'=2] {'wide'}, use_global_device_ids=true, to_apply=%region_11.13 | all-reduce | flops 2304 | bytes 18432 | tf_op jit(solution)/shard_map/psum | solution.py:51
  409.1 4.4 cholesky.81
  414.9 3.7 custom-call.13
  418.7 2.0 fusion.5
  422.3 55.6 %reduce-scatter.17.cloned.1.call-done = f32[144,48]{1,0:T(8,128)} async-done(((f32[2304,48]{1,0:T(8,128)}), f32[144,48]{1,0:T(8,128)}) %reduce-scatter.17.cloned.1.call-update) | async-done | bytes 27664
  477.9 1.6 copy.44
  (58 shorter events, 21.2 us)
Async XLA Ops:
  7.2 1.4 copy-start
  7.2 4.5 copy-start.3
  7.2 74.7 %reduce-scatter.11.cloned.1.call-start = ((), (), s32[]{:S(2)}) async-start(), calls=%async_computation.4 | async-start | bytes 1327104 | tf_op jit(solution)/shard_map/reduce_scatter | solution.py:33
  11.7 70.2 %copy-start.7 = (f32[64,48]{0,1:T(8,128)S(1)}, f32[64,48]{0,1:T(8,128)}, u32[]{:S(2)}) copy-start(f32[64,48]{0,1:T(8,128)} %param.6) | copy-start | bytes 36868
  13.9 186.2 %reduce-scatter.13.cloned.1.call-start = ((), (), s32[]{:S(2)}) async-start(), calls=%async_computation.5 | async-start | bytes 1253376
  135.9 1.1 copy-start.1
  136.0 1.1 copy-start.5
  144.5 200.6 %reduce-scatter.15.cloned.1.call-start = ((), (), s32[]{:S(2)}) async-start(), calls=%async_computation.6 | async-start | bytes 1253376
  276.2 6.3 %copy-start.2 = (f32[64,48]{0,1:T(8,128)S(1)}, f32[64,48]{0,1:T(8,128)}, u32[]{:S(2)}) copy-start(f32[64,48]{0,1:T(8,128)} %copy-done.1) | copy-start | bytes 36868
  280.2 4.5 copy-start.4
  288.2 189.7 %reduce-scatter.17.cloned.1.call-start = ((), (), s32[]{:S(2)}) async-start(), calls=%async_computation.7 | async-start | bytes 1253376
  418.7 3.6 copy-start.6
Sparse Core Ops, SparseCore 0:
  14.0 67.8 reduce-scatter.10
  144.7 55.3 reduce-scatter.12
  288.3 56.7 reduce-scatter.14
  422.4 55.4 reduce-scatter.16
